TPU v7x, 512 devices: a whole 4x8x8 slice. The times are simulated.
512 devices in a mesh: graph: 16 (over y, z_lo), gr: 4 (over z_hi), gc: 8 (over x, core).
Axes of the slice: x: 4, y: 8, z: 8 (z_hi: 4, z_lo: 2; z = z_hi * 2 + z_lo), core: 2. Of those that a mesh axis runs over, the one named last changes fastest.
Arguments:
- x_in: bfloat16 [8192, 256], P(('graph', 'gr', 'gc')), parts along dimension 0, may hold values from -64 to 64
- node_type: int32 [8192], P(('graph', 'gr', 'gc')), parts along dimension 0, may hold values from 0 to 7
- node_mask: int32 [8192], P(('graph', 'gr', 'gc')), parts along dimension 0, may hold values 0 or 1
- adj_cat: int32 [8192, 512], P(('graph', 'gc'), 'gr'), parts along dimension 0, may hold values from 0 to 4
- ori_cat: int32 [8192, 512], P(('graph', 'gc'), 'gr'), parts along dimension 0, may hold values from 0 to 7
- type_table: float32 [8, 256], replicated, may hold values from -6 to 6
- adj_table: float32 [5, 32], replicated, may hold values from -6 to 6
- ori_table: float32 [8, 32], replicated, may hold values from -6 to 6
- w_qkv: bfloat16 [256, 768], replicated, may hold values from -1.5 to 1.5
- w_film: bfloat16 [32, 512], replicated, may hold values from -0.75 to 0.75
- w_edge_out: bfloat16 [256, 32], replicated, may hold values from -0.375 to 0.375
- w_node_out: bfloat16 [256, 256], replicated, may hold values from -0.375 to 0.375
- w_node_up: bfloat16 [256, 512], replicated, may hold values from -0.375 to 0.375
- w_node_down: bfloat16 [512, 256], replicated, may hold values from -0.25 to 0.25
- w_edge_up: bfloat16 [32, 128], replicated, may hold values from -1 to 1
- w_edge_down: bfloat16 [128, 32], replicated, may hold values from -0.5 to 0.5
- node_gain1: float32 [256], replicated, may hold values from 0.25 to 1.75
- node_gain2: float32 [256], replicated, may hold values from 0.25 to 1.75
- edge_gain1: float32 [32], replicated, may hold values from 0.25 to 1.75
- edge_gain2: float32 [32], replicated, may hold values from 0.25 to 1.75
Outputs:
- node_out: bfloat16 [8192, 256], P(('graph', 'gr', 'gc')), parts along dimension 0
- edge_out: bfloat16 [32, 8192, 512], P(None, ('graph', 'gc'), 'gr'), parts along dimension 1
There are 16 independent parts, one for each index of `graph`. A program takes and returns all parts, laid end to end along the dimension named above; an argument that names none is the same for every part. Nothing has to cross between parts.
All inputs are finite; a program needn't handle non-finite values. No bound on the sum of `node_mask` on one device may be relied on, other than what follows from the above.
Results may differ from a plain program's by a relative error of at most 0.0075.
The roundings to bfloat16 on the way count: a program that leaves them out, or rounds other values in their place, can miss the bound.
Values may be sent and summed in bfloat16 or wider, within the bound.
A program may use at most 64 MiB of HBM per device.

v0:
```python
import math
import jax
import jax.numpy as jnp
from jax import lax
from jax.sharding import PartitionSpec as P

HEAD_DIM = 32


def combined_all(value, axis, join):
    pieces = jax.tree.map(lambda part: lax.all_gather(part, axis), value)
    head = jax.tree.map(lambda part: part[0], pieces)
    tail = jax.tree.map(lambda part: part[1:], pieces)
    running, _ = lax.scan(lambda running, slab: (join(running, slab), None), head, tail)
    return running


def layer_norm(values, gain, axis):
    center = values - jnp.mean(values, axis=axis, keepdims=True)
    spread = jnp.mean(center * center, axis=axis, keepdims=True)
    return center / jnp.sqrt(spread + 1e-05) * gain


def combine_stats(earlier, later):
    peak = jnp.maximum(earlier[0], later[0])
    first_factor = jnp.exp(earlier[0] - peak)
    second_factor = jnp.exp(later[0] - peak)
    return (
        peak,
        earlier[1] * first_factor + later[1] * second_factor,
        earlier[2] * first_factor + later[2] * second_factor,
    )


def category_sum(codes, lookup):
    levels = jnp.arange(lookup.shape[0], dtype=jnp.int32)
    onehot = (codes[None] == levels[:, None, None]).astype(jnp.float32)
    return jnp.einsum("acr,af->fcr", onehot, lookup, precision=lax.Precision.HIGHEST)


def body(
    x_in,
    node_type,
    node_mask,
    adj_cat,
    ori_cat,
    type_table,
    adj_table,
    ori_table,
    w_qkv,
    w_film,
    w_edge_out,
    w_node_out,
    w_node_up,
    w_node_down,
    w_edge_up,
    w_edge_down,
    node_gain1,
    node_gain2,
    edge_gain1,
    edge_gain2,
):
    width = w_node_out.shape[0]
    owned = x_in.shape[0]
    col_count, row_count = adj_cat.shape
    column_index = lax.axis_index("gc")
    type_levels = jnp.arange(type_table.shape[0], dtype=jnp.int32)
    type_onehot = (node_type[:, None] == type_levels[None, :]).astype(jnp.float32)
    embedded = jnp.dot(type_onehot, type_table, precision=lax.Precision.HIGHEST)
    nodes0 = (x_in.astype(jnp.float32) + embedded).astype(jnp.bfloat16)
    projected = jnp.dot(nodes0, w_qkv, preferred_element_type=jnp.float32).astype(jnp.bfloat16)
    query_own = projected[:, :width]
    key_own = projected[:, width : 2 * width]
    value_own = projected[:, 2 * width :]
    valid_own = node_mask.astype(jnp.bfloat16)
    query_rows, valid_rows = (
        lax.all_gather(query_own, "gc", axis=0, tiled=True),
        lax.all_gather(valid_own, "gc", axis=0, tiled=True),
    )
    key_all, value_all, valid_all = (
        lax.all_gather(key_own, ("gr", "gc"), axis=0, tiled=True),
        lax.all_gather(value_own, ("gr", "gc"), axis=0, tiled=True),
        lax.all_gather(valid_own, ("gr", "gc"), axis=0, tiled=True),
    )
    first_col = column_index * col_count
    key_cols = lax.dynamic_slice_in_dim(key_all, first_col, col_count, 0)
    value_cols = lax.dynamic_slice_in_dim(value_all, first_col, col_count, 0)
    valid_cols = lax.dynamic_slice_in_dim(valid_all, first_col, col_count, 0)
    edges0 = (category_sum(adj_cat, adj_table) + category_sum(ori_cat, ori_table)).astype(
        jnp.bfloat16
    )
    edge_width = edges0.shape[0]
    score_scale = 1.0 / math.sqrt(HEAD_DIM)
    query_t = query_rows.astype(jnp.float32).T
    key_block = min(16, col_count)
    turns = col_count // key_block

    def sweep(turn, state):
        peak, summed, weighted, messages = state
        begin_at = turn * key_block
        edge_part = lax.dynamic_slice_in_dim(edges0, begin_at, key_block, 1)
        film = jnp.einsum("fjr,fk->kjr", edge_part, w_film, preferred_element_type=jnp.float32)
        key_part = lax.dynamic_slice_in_dim(key_cols, begin_at, key_block, 0).astype(jnp.float32).T
        value_part = (
            lax.dynamic_slice_in_dim(value_cols, begin_at, key_block, 0).astype(jnp.float32).T
        )
        valid_part = lax.dynamic_slice_in_dim(valid_cols, begin_at, key_block, 0)
        scores = (
            key_part[:, :, None] * query_t[:, None, :] * score_scale * (film[:width] + 1.0)
            + film[width:]
        )
        message = jnp.einsum(
            "cjr,cf->fjr",
            scores.astype(jnp.bfloat16),
            w_edge_out,
            preferred_element_type=jnp.float32,
        )
        masked = jnp.where(valid_part[None, :, None] > 0, scores, -1000000000.0)
        new_peak = jnp.maximum(peak, jnp.max(masked, axis=1))
        factor = jnp.exp(peak - new_peak)
        expo = jnp.exp(masked - new_peak[:, None, :])
        summed = summed * factor + jnp.sum(expo, axis=1)
        weighted = weighted * factor + jnp.sum(expo * value_part[:, :, None], axis=1)
        messages = lax.dynamic_update_slice_in_dim(messages, message, begin_at, 1)
        return (new_peak, summed, weighted, messages)

    initial = (
        jnp.full((width, row_count), -1e30, jnp.float32),
        jnp.zeros((width, row_count), jnp.float32),
        jnp.zeros((width, row_count), jnp.float32),
        jnp.zeros((edge_width, col_count, row_count), jnp.float32),
    )
    peak, summed, weighted, messages = lax.fori_loop(0, turns, sweep, initial)
    peak, summed, weighted = combined_all((peak, summed, weighted), "gc", combine_stats)
    attended = lax.dynamic_slice_in_dim(weighted / summed, column_index * owned, owned, 1).T
    valid_node = valid_own.astype(jnp.float32)
    attn_bf = attended.astype(jnp.bfloat16)
    nodes1 = layer_norm(
        nodes0.astype(jnp.float32)
        + jnp.dot(attn_bf, w_node_out, preferred_element_type=jnp.float32),
        node_gain1,
        -1,
    ).astype(jnp.bfloat16)
    hidden_node = jnp.maximum(
        jnp.dot(nodes1, w_node_up, preferred_element_type=jnp.float32), 0.0
    ).astype(jnp.bfloat16)
    node_out = (
        layer_norm(
            nodes1.astype(jnp.float32)
            + jnp.dot(hidden_node, w_node_down, preferred_element_type=jnp.float32),
            node_gain2,
            -1,
        )
        * valid_node[:, None]
    ).astype(jnp.bfloat16)
    edges1 = layer_norm(edges0.astype(jnp.float32) + messages, edge_gain1[:, None, None], 0).astype(
        jnp.bfloat16
    )
    hidden_edge = jnp.maximum(
        jnp.einsum("fjr,fh->hjr", edges1, w_edge_up, preferred_element_type=jnp.float32), 0.0
    ).astype(jnp.bfloat16)
    edges2 = layer_norm(
        edges1.astype(jnp.float32)
        + jnp.einsum("hjr,hf->fjr", hidden_edge, w_edge_down, preferred_element_type=jnp.float32),
        edge_gain2[:, None, None],
        0,
    )
    edge_out = (
        edges2
        * valid_cols.astype(jnp.float32)[None, :, None]
        * valid_rows.astype(jnp.float32)[None, None, :]
    ).astype(jnp.bfloat16)
    return (node_out, edge_out)


def solution(mesh):
    return jax.shard_map(
        body,
        mesh=mesh,
        in_specs=(
            P(("graph", "gr", "gc"), None),
            P(("graph", "gr", "gc")),
            P(("graph", "gr", "gc")),
            P(("graph", "gc"), "gr"),
            P(("graph", "gc"), "gr"),
            P(),
            P(),
            P(),
            P(),
            P(),
            P(),
            P(),
            P(),
            P(),
            P(),
            P(),
            P(),
            P(),
            P(),
            P(),
        ),
        out_specs=(P(("graph", "gr", "gc"), None), P(None, ("graph", "gc"), "gr")),
        check_vma=False,
    )
```

profile of v0, /device:TPU:1, one launch (start us, length us, event | category | flops | bytes accessed | tf_op | source)
XLA Modules:
  0.0 318.0 jit_solution(9639753481749543636)
XLA Ops:
  7.3 1.2 convert_convert_fusion
  8.5 1.3 dynamic-slice
  10.7 76.1 %all-reduce = bf16[512]{0:T(512)(128)(2,1)S(1)} all-reduce(bf16[512]{0:T(512)(128)(2,1)S(1)} %dynamic-update-slice), channel_id=1, replica_groups=mesh['graph'=16,'gr'=4,'gc'=8] {'gr','gc'}, use_global_device_ids=true, to_apply=%add | all-reduce | flops 512 | bytes 2048
  88.3 45.3 %all_gather.36 = bf16[512,256]{1,0:T(8,128)(2,1)S(1)} all-gather(bf16[16,256]{1,0:T(8,128)(2,1)S(1)} %get-tuple-element.348), channel_id=1, replica_groups=mesh['graph'=16,'gr'=4,'gc'=8] {'gr','gc'}, dimensions={0}, use_global_device_ids=true | all-gather | bytes 270336 | tf_op jit(solution)/shard_map/all_gather | solution.py:82
  134.9 41.5 %all_gather.34 = bf16[512,256]{1,0:T(8,128)(2,1)S(1)} all-gather(bf16[16,256]{1,0:T(8,128)(2,1)S(1)} %get-tuple-element.350), channel_id=1, replica_groups=mesh['graph'=16,'gr'=4,'gc'=8] {'gr','gc'}, dimensions={0}, use_global_device_ids=true | all-gather | bytes 270336 | tf_op jit(solution)/shard_map/all_gather | solution.py:81
  177.0 12.7 %all_gather.35 = bf16[128,256]{1,0:T(8,128)(2,1)S(1)} all-gather(bf16[16,256]{1,0:T(8,128)(2,1)S(1)} %get-tuple-element.349), channel_id=1, replica_groups=mesh['graph'=16,'gr'=4,'gc'=8] {'gc'}, dimensions={0}, use_global_device_ids=true | all-gather | bytes 73728 | tf_op jit(solution)/shard_map/all_gather | solution.py:77
  190.4 1.4 fusion.32
  192.4 1.1 broadcast_in_dim.67
  193.5 24.5 %while.35 = (s32[]{:T(128)}, f32[256,128]{0,1:T(8,128)S(1)}, f32[256,128]{0,1:T(8,128)S(1)}, f32[256,128]{0,1:T(8,128)S(1)}, f32[32,64,128]{2,0,1:T(8,128)}, /*i...) while((s32[]{:T(128)}, f32[256,128]{0,1:T(8,128)S(1)}, ...), condition=%wide.region_4.5_spmd.clone, body=%wide.region_0.4_spmd.clone.sunk | while | flops 107716664 | bytes 18153920 | solution.py:133
  194.3 1.5 convolution_bitcast_fusion.3
  197.2 1.1 fusion.81
  198.3 1.2 multiply_reduce_fusion.6
  200.4 1.5 convolution_bitcast_fusion.3
  204.5 1.2 multiply_reduce_fusion.6
  206.5 1.5 convolution_bitcast_fusion.3
  209.5 1.1 fusion.81
  210.6 1.2 multiply_reduce_fusion.6
  212.7 1.5 convolution_bitcast_fusion.3
  216.7 1.2 multiply_reduce_fusion.6
  220.6 1.5 fusion.31
  222.0 1.3 dynamic-slice.1
  224.2 11.9 %all-reduce.1 = bf16[128]{0:T(256)(128)(2,1)S(1)} all-reduce(bf16[128]{0:T(256)(128)(2,1)S(1)} %dynamic-update-slice.1), channel_id=1, replica_groups=mesh['graph'=16,'gr'=4,'gc'=8] {'gc'}, use_global_device_ids=true, to_apply=%add.1 | all-reduce | flops 128 | bytes 512
  236.2 1.5 multiply_reduce_fusion.2
  237.8 2.6 fusion.57
  243.1 1.2 slice.66
  244.3 29.6 %all-gather.9.cloned.1.call-done = f32[2048,128]{1,0:T(8,128)} async-done(((f32[256,128]{1,0:T(8,128)}), f32[2048,128]{1,0:T(8,128)}) %all-gather.9.cloned.1.call-update) | async-done | bytes 1048592 | tf_op jit(solution)/shard_map/all_gather | solution.py:11
  273.9 1.3 slice.67
  275.2 29.4 %all-gather.11.cloned.1.call-done = f32[2048,128]{1,0:T(8,128)} async-done(((f32[256,128]{1,0:T(8,128)}), f32[2048,128]{1,0:T(8,128)}) %all-gather.11.cloned.1.call-update) | async-done | bytes 1048592 | tf_op jit(solution)/shard_map/all_gather | solution.py:11
  304.6 1.3 slice.68
  305.9 1.6 while.34
  307.6 1.3 fusion.55
  309.1 1.5 fusion.56
  (145 shorter events, 24.1 us)
Async XLA Ops:
  7.2 80.6 %copy-start = (bf16[256,768]{1,0:T(8,128)(2,1)S(1)}, bf16[256,768]{1,0:T(8,128)(2,1)}, u32[]{:S(2)}) copy-start(bf16[256,768]{1,0:T(8,128)(2,1)} %param.32) | copy-start | bytes 1179652
  7.2 184.6 %copy-start.4 = (s32[64,128]{1,0:T(8,128)S(1)}, s32[64,128]{1,0:T(8,128)}, u32[]{:S(2)}) copy-start(s32[64,128]{1,0:T(8,128)} %param.28) | copy-start | bytes 98308
  7.2 184.6 %copy-start.7 = (f32[8,32]{1,0:T(8,128)S(1)}, f32[8,32]{1,0:T(8,128)}, u32[]{:S(2)}) copy-start(f32[8,32]{1,0:T(8,128)} %param.31) | copy-start | bytes 3076
  7.2 235.9 %all-gather.7.cloned.1.call-start = ((), (), s32[]{:S(2)}) async-start(), calls=%async_computation | async-start | bytes 1179648 | tf_op jit(solution)/shard_map/all_gather | solution.py:11
  8.5 78.3 %copy-start.15 = (bf16[16]{0:T(256)(128)(2,1)}, bf16[16]{0:T(256)(128)(2,1)S(1)}, u32[]{:S(2)}) copy-start(bf16[16]{0:T(256)(128)(2,1)S(1)} %get-tuple-element.352) | copy-start | bytes 100
  87.7 0.6 copy-start.5
  194.3 2.2 copy-start.1
  196.5 0.5 copy-start.3
  196.5 0.7 copy-start.2
  200.4 2.2 copy-start.1
  202.6 0.5 copy-start.3
  202.6 0.7 copy-start.2
  206.5 2.2 copy-start.1
  208.7 0.5 copy-start.3
  208.7 0.7 copy-start.2
  212.7 2.2 copy-start.1
  214.9 0.5 copy-start.3
  214.9 0.7 copy-start.2
  218.1 5.9 %copy-start.16 = (bf16[16]{0:T(256)(128)(2,1)S(1)}, bf16[16]{0:T(256)(128)(2,1)}, u32[]{:S(2)}) copy-start(bf16[16]{0:T(256)(128)(2,1)} %copy-done.15) | copy-start | bytes 100
  218.9 18.9 %copy-start.12 = (bf16[32,128]{1,0:T(8,128)(2,1)S(1)}, bf16[32,128]{1,0:T(8,128)(2,1)}, u32[]{:S(2)}) copy-start(bf16[32,128]{1,0:T(8,128)(2,1)} %param.38) | copy-start | bytes 24580
  218.9 18.9 %copy-start.13 = (bf16[128,32]{0,1:T(8,128)(2,1)S(1)}, bf16[128,32]{0,1:T(8,128)(2,1)}, u32[]{:S(2)}) copy-start(bf16[128,32]{0,1:T(8,128)(2,1)} %param.39) | copy-start | bytes 24580
  218.9 18.9 %copy-start.14 = (f32[32]{0:T(128)S(1)}, f32[32]{0:T(128)}, u32[]{:S(2)}) copy-start(f32[32]{0:T(128)} %param.42) | copy-start | bytes 388
  218.9 55.0 %all-gather.9.cloned.1.call-start = ((), (), s32[]{:S(2)}) async-start(), calls=%async_computation.1 | async-start | bytes 1179648 | tf_op jit(solution)/shard_map/all_gather | solution.py:11
  219.7 84.9 %all-gather.11.cloned.1.call-start = ((), (), s32[]{:S(2)}) async-start(), calls=%async_computation.2 | async-start | bytes 1179648 | tf_op jit(solution)/shard_map/all_gather | solution.py:11
  237.8 2.9 copy-start.8
  237.8 2.9 copy-start.10
  244.3 61.5 %slice-start = ((f32[2048,128]{1,0:T(8,128)}), f32[256,128]{1,0:T(8,128)S(1)}, s32[]{:S(2)}) async-start(f32[2048,128]{1,0:T(8,128)} %all-gather.7.cloned.1.call-done), calls=%async_computation.3 | async-start | bytes 262144 | tf_op jit(solution)/shard_map/slice | solution.py:12
  273.9 32.0 %slice-start.1 = ((f32[2048,128]{1,0:T(8,128)}), f32[256,128]{1,0:T(8,128)S(1)}, s32[]{:S(2)}) async-start(f32[2048,128]{1,0:T(8,128)} %all-gather.9.cloned.1.call-done), calls=%async_computation.4 | async-start | bytes 262144 | tf_op jit(solution)/shard_map/slice | solution.py:12
  304.6 1.3 slice-start.2
  305.9 1.7 copy-start.6
  305.9 4.9 %copy-start.9 = (f32[256]{0:T(256)S(1)}, f32[256]{0:T(256)}, u32[]{:S(2)}) copy-start(f32[256]{0:T(256)} %param.41) | copy-start | bytes 3076
  305.9 4.9 %copy-start.11 = (f32[16]{0:T(128)S(1)}, f32[16]{0:T(128)}, u32[]{:S(2)}) copy-start(f32[16]{0:T(128)} %get-tuple-element.351) | copy-start | bytes 196
Sparse Core Ops, SparseCore 0:
  219.0 24.0 all-gather.6
  245.2 28.6 all-gather.8
  276.1 28.4 all-gather.10
where the time goes:
time: 319 us; the launch traced here: 318 us
  blocking collectives  188 us (59%)
  waiting for transfers between devices  60.1 us (19%)
  other arithmetic  21.5 us (7%)
  matrix products  19.1 us (6%)
  between operations  15.5 us (5%)
  local copies, waits for them, and re-layouts  13.8 us (4%)
    unnamed x2, blocking collectives  88.1 us
    all_gather x3, waiting for transfers between devices, combined_all(): pieces = jax.tree.map(lambda part: lax.all_gather(part, axis), value)  60 us
    all_gather x1, blocking collectives, body(): lax.all_gather(value_own, ('gr', 'gc'), axis=0, tiled=True)  45.3 us
    all_gather x1, blocking collectives, body(): lax.all_gather(key_own, ('gr', 'gc'), axis=0, tiled=True)  41.5 us
    all_gather x1, blocking collectives, body(): lax.all_gather(query_own, 'gc', axis=0, tiled=True)  12.7 us
  transfers between devices with their start and end apart: 3, of which 3 were waited for; matrix products, arithmetic and copies ran while one was open for 4% of the time, Pallas kernels for 0%

commit v1 on v0

--- a/solution.py
+++ b/solution.py
@@ -5,6 +5,11 @@
 from jax.sharding import PartitionSpec as P
 
 HEAD_DIM = 32
+
+
+def all_by_exchange(array, name, dim):
+    sent = jnp.stack([array] * lax.axis_size(name))
+    return jnp.concatenate(lax.all_to_all(sent, name, 0, 0), axis=dim)
 
 
 def combined_all(value, axis, join):
@@ -74,7 +79,7 @@
     value_own = projected[:, 2 * width :]
     valid_own = node_mask.astype(jnp.bfloat16)
     query_rows, valid_rows = (
-        lax.all_gather(query_own, "gc", axis=0, tiled=True),
+        all_by_exchange(query_own, "gc", 0),
         lax.all_gather(valid_own, "gc", axis=0, tiled=True),
     )
     key_all, value_all, valid_all = (

time: 319 us -> 312 us (0.978)
  blocking collectives: 188 us -> 170 us
  starting transfers between devices: 0.12 us -> 10.2 us
    all_gather x1 -> x0, blocking collectives: 12.7 us -> none  [body(): lax.all_gather(query_own, 'gc', axis=0, tiled=True)]
    all_to_all x0 -> x1, starting transfers between devices: none -> 10.1 us  [all_by_exchange(): return jnp.concatenate(lax.all_to_all(sent, name, 0, 0), axis=dim)]
    unnamed x2, blocking collectives: 88.1 us -> 82.8 us
  transfers between devices with their start and end apart: 3 -> 4, of which waited for: 3 -> 2; matrix products, arithmetic and copies ran while one was open for 4% -> 6% of each run, Pallas kernels for 0% -> 0%
where the time goes in v1:
time: 312 us; the launch traced here: 311 us
  blocking collectives  170 us (54%)
  waiting for transfers between devices  58.7 us (19%)
  other arithmetic  21.9 us (7%)
  matrix products  19.1 us (6%)
  between operations  15.4 us (5%)
  local copies, waits for them, and re-layouts  15.1 us (5%)
  starting transfers between devices  10.2 us (3%)
    unnamed x2, blocking collectives  82.8 us
    all_gather x3, waiting for transfers between devices, combined_all(): pieces = jax.tree.map(lambda part: lax.all_gather(part, axis), value)  58.6 us
    all_gather x1, blocking collectives, body(): lax.all_gather(value_own, ('gr', 'gc'), axis=0, tiled=True)  45.6 us
    all_gather x1, blocking collectives, body(): lax.all_gather(key_own, ('gr', 'gc'), axis=0, tiled=True)  41.5 us
    all_to_all x1, starting transfers between devices, all_by_exchange(): return jnp.concatenate(lax.all_to_all(sent, name, 0, 0), axis=dim)  10.1 us
  transfers between devices with their start and end apart: 4, of which 2 were waited for; matrix products, arithmetic and copies ran while one was open for 6% of the time, Pallas kernels for 0%

profile of v1, /device:TPU:1, one launch (start us, length us, event | category | flops | bytes accessed | tf_op | source)
XLA Modules:
  0.0 310.5 jit_solution(11889700111484591801)
XLA Ops:
  9.4 10.1 %all-to-all-start = ((bf16[8,16,256]{2,1,0:T(8,128)(2,1)}), bf16[8,16,256]{2,1,0:T(8,128)(2,1)S(1)}, u32[]{:S(2)}, u32[]{:S(2)}) async-start(bf16[8,16,256]{2,1,0:T(8,128)(2,1)} %stack.2), calls=%async_computation | async-start | bytes 131072 | tf_op jit(solution)/shard_map/all_to_all | solution.py:12
  19.6 1.1 convert_convert_fusion
  20.7 1.3 dynamic-slice
  23.0 70.8 %all-reduce = bf16[512]{0:T(512)(128)(2,1)S(1)} all-reduce(bf16[512]{0:T(512)(128)(2,1)S(1)} %dynamic-update-slice), channel_id=1, replica_groups=mesh['graph'=16,'gr'=4,'gc'=8] {'gr','gc'}, use_global_device_ids=true, to_apply=%add | all-reduce | flops 512 | bytes 2048
  93.8 45.6 %all_gather.32 = bf16[512,256]{1,0:T(8,128)(2,1)S(1)} all-gather(bf16[16,256]{1,0:T(8,128)(2,1)S(1)} %get-tuple-element.348), channel_id=1, replica_groups=mesh['graph'=16,'gr'=4,'gc'=8] {'gr','gc'}, dimensions={0}, use_global_device_ids=true | all-gather | bytes 270336 | tf_op jit(solution)/shard_map/all_gather | solution.py:87
  139.4 41.5 %all_gather.31 = bf16[512,256]{1,0:T(8,128)(2,1)S(1)} all-gather(bf16[16,256]{1,0:T(8,128)(2,1)S(1)} %get-tuple-element.350), channel_id=1, replica_groups=mesh['graph'=16,'gr'=4,'gc'=8] {'gr','gc'}, dimensions={0}, use_global_device_ids=true | all-gather | bytes 270336 | tf_op jit(solution)/shard_map/all_gather | solution.py:86
  182.1 1.4 fusion.32
  185.4 1.1 broadcast_in_dim.67
  186.6 24.9 %while.35 = (s32[]{:T(128)}, f32[256,128]{0,1:T(8,128)S(1)}, f32[256,128]{0,1:T(8,128)S(1)}, f32[256,128]{0,1:T(8,128)S(1)}, f32[32,64,128]{2,0,1:T(8,128)}, /*i...) while((s32[]{:T(128)}, f32[256,128]{0,1:T(8,128)S(1)}, ...), condition=%wide.region_4.5_spmd.clone, body=%wide.region_0.4_spmd.clone.sunk | while | flops 107716664 | bytes 18153920 | solution.py:138
  187.3 1.5 convolution_bitcast_fusion.3
  190.3 1.1 fusion.81
  191.4 1.2 multiply_reduce_fusion.6
  193.5 1.5 convolution_bitcast_fusion.3
  197.6 1.2 multiply_reduce_fusion.6
  199.8 1.5 convolution_bitcast_fusion.3
  202.7 1.1 fusion.81
  203.9 1.2 multiply_reduce_fusion.6
  206.0 1.5 convolution_bitcast_fusion.3
  210.1 1.2 multiply_reduce_fusion.6
  213.2 1.3 dynamic-slice.1
  215.9 11.9 %all-reduce.1 = bf16[128]{0:T(256)(128)(2,1)S(1)} all-reduce(bf16[128]{0:T(256)(128)(2,1)S(1)} %dynamic-update-slice.1), channel_id=1, replica_groups=mesh['graph'=16,'gr'=4,'gc'=8] {'gc'}, use_global_device_ids=true, to_apply=%add.1 | all-reduce | flops 128 | bytes 512
  228.6 1.5 fusion.31
  230.1 1.5 multiply_reduce_fusion.2
  231.7 2.6 fusion.57
  235.9 1.2 slice.66
  237.2 29.2 %all-gather.9.cloned.1.call-done = f32[2048,128]{1,0:T(8,128)} async-done(((f32[256,128]{1,0:T(8,128)}), f32[2048,128]{1,0:T(8,128)}) %all-gather.9.cloned.1.call-update) | async-done | bytes 1048592 | tf_op jit(solution)/shard_map/all_gather | solution.py:16
  266.4 1.3 slice.67
  267.7 29.4 %all-gather.11.cloned.1.call-done = f32[2048,128]{1,0:T(8,128)} async-done(((f32[256,128]{1,0:T(8,128)}), f32[2048,128]{1,0:T(8,128)}) %all-gather.11.cloned.1.call-update) | async-done | bytes 1048592 | tf_op jit(solution)/shard_map/all_gather | solution.py:16
  297.1 1.3 slice.68
  298.4 1.6 while.34
  300.1 1.3 fusion.55
  301.6 1.5 fusion.56
  (145 shorter events, 24.5 us)
Async XLA Ops:
  7.2 1.0 copy-start
  7.2 176.3 %copy-start.4 = (s32[64,128]{1,0:T(8,128)S(1)}, s32[64,128]{1,0:T(8,128)}, u32[]{:S(2)}) copy-start(s32[64,128]{1,0:T(8,128)} %param.28) | copy-start | bytes 98308
  7.2 176.3 %copy-start.7 = (f32[8,32]{1,0:T(8,128)S(1)}, f32[8,32]{1,0:T(8,128)}, u32[]{:S(2)}) copy-start(f32[8,32]{1,0:T(8,128)} %param.31) | copy-start | bytes 3076
  8.2 0.6 copy-start.5
  9.4 175.3 %all-to-all-start = ((bf16[8,16,256]{2,1,0:T(8,128)(2,1)}), bf16[8,16,256]{2,1,0:T(8,128)(2,1)S(1)}, u32[]{:S(2)}, u32[]{:S(2)}) async-start(bf16[8,16,256]{2,1,0:T(8,128)(2,1)} %stack.2), calls=%async_computation | async-start | bytes 131072 | tf_op jit(solution)/shard_map/all_to_all | solution.py:12
  19.5 216.4 %all-gather.7.cloned.1.call-start = ((), (), s32[]{:S(2)}) async-start(), calls=%async_computation.1 | async-start | bytes 1179648 | tf_op jit(solution)/shard_map/all_gather | solution.py:16
  20.7 118.7 %copy-start.15 = (bf16[16]{0:T(256)(128)(2,1)}, bf16[16]{0:T(256)(128)(2,1)S(1)}, u32[]{:S(2)}) copy-start(bf16[16]{0:T(256)(128)(2,1)S(1)} %get-tuple-element.352) | copy-start | bytes 100
  187.3 2.3 copy-start.1
  189.5 0.6 copy-start.3
  189.5 0.7 copy-start.2
  193.5 2.3 copy-start.1
  195.8 0.6 copy-start.3
  195.8 0.7 copy-start.2
  199.8 2.3 copy-start.1
  202.0 0.6 copy-start.3
  202.0 0.7 copy-start.2
  206.0 2.3 copy-start.1
  208.3 0.6 copy-start.3
  208.3 0.7 copy-start.2
  212.2 54.1 %all-gather.9.cloned.1.call-start = ((), (), s32[]{:S(2)}) async-start(), calls=%async_computation.2 | async-start | bytes 1179648 | tf_op jit(solution)/shard_map/all_gather | solution.py:16
  212.3 19.4 %copy-start.12 = (bf16[32,128]{1,0:T(8,128)(2,1)S(1)}, bf16[32,128]{1,0:T(8,128)(2,1)}, u32[]{:S(2)}) copy-start(bf16[32,128]{1,0:T(8,128)(2,1)} %param.38) | copy-start | bytes 24580
  212.3 19.4 %copy-start.13 = (bf16[128,32]{0,1:T(8,128)(2,1)S(1)}, bf16[128,32]{0,1:T(8,128)(2,1)}, u32[]{:S(2)}) copy-start(bf16[128,32]{0,1:T(8,128)(2,1)} %param.39) | copy-start | bytes 24580
  212.3 19.4 %copy-start.14 = (f32[32]{0:T(128)S(1)}, f32[32]{0:T(128)}, u32[]{:S(2)}) copy-start(f32[32]{0:T(128)} %param.42) | copy-start | bytes 388
  213.1 84.0 %all-gather.11.cloned.1.call-start = ((), (), s32[]{:S(2)}) async-start(), calls=%async_computation.3 | async-start | bytes 1179648 | tf_op jit(solution)/shard_map/all_gather | solution.py:16
  231.7 2.9 copy-start.8
  231.7 2.9 copy-start.10
  237.2 61.2 %slice-start = ((f32[2048,128]{1,0:T(8,128)}), f32[256,128]{1,0:T(8,128)S(1)}, s32[]{:S(2)}) async-start(f32[2048,128]{1,0:T(8,128)} %all-gather.7.cloned.1.call-done), calls=%async_computation.4 | async-start | bytes 262144 | tf_op jit(solution)/shard_map/slice | solution.py:17
  266.4 32.0 %slice-start.1 = ((f32[2048,128]{1,0:T(8,128)}), f32[256,128]{1,0:T(8,128)S(1)}, s32[]{:S(2)}) async-start(f32[2048,128]{1,0:T(8,128)} %all-gather.9.cloned.1.call-done), calls=%async_computation.5 | async-start | bytes 262144 | tf_op jit(solution)/shard_map/slice | solution.py:17
  297.1 1.3 slice-start.2
  298.4 1.7 copy-start.6
  298.4 4.9 %copy-start.9 = (f32[256]{0:T(256)S(1)}, f32[256]{0:T(256)}, u32[]{:S(2)}) copy-start(f32[256]{0:T(256)} %param.41) | copy-start | bytes 3076
  298.4 4.9 %copy-start.11 = (f32[16]{0:T(128)S(1)}, f32[16]{0:T(128)}, u32[]{:S(2)}) copy-start(f32[16]{0:T(128)} %get-tuple-element.351) | copy-start | bytes 196
Sparse Core Ops, SparseCore 0:
  212.4 23.3 all-gather.6
  237.9 28.4 all-gather.8
  268.6 28.4 all-gather.10
